TPU v7x, 32 devices: a whole 2x2x4 slice. The times are simulated.
32 devices in a mesh: dp: 2 (over core), seq: 4 (over y, x), head: 4 (over z).
Axes of the slice: x: 2, y: 2, z: 4, core: 2. Of those that a mesh axis runs over, the one named last changes fastest.
Arguments:
- query_rows: bfloat16 [2, 2048, 4096], P('dp', 'seq', 'head'), may hold values from -1.796875 to 1.796875
- key_rows: bfloat16 [2, 2048, 4096], P('dp', 'seq', 'head'), may hold values from -1.796875 to 1.796875
- value_rows: bfloat16 [2, 2048, 4096], P('dp', 'seq', 'head'), may hold values from -6 to 6
- norm_gain: float32 [4096], P('head'), may hold values from 0.1 to 1.9
- cotangent: bfloat16 [2, 2048, 4096], P('dp', 'seq', 'head'), may hold values from -10 to 10
- loss_mask: int32 [2, 2048], P('dp', 'seq'), may hold values 0 or 1
- importance: float32 [2, 2048], P('dp', 'seq'), may hold values from 0.5 to 2
- advantage: float32 [2], P('dp'), may hold values from -3 to 3
- lengths: int32 [2], P('dp'), may hold values from 512 to 2048, as said below
- decay_index: int32 [32], P('head'), may hold values from 0 to 11
Outputs:
- mixed: bfloat16 [2, 2048, 4096], P('dp', 'seq', 'head')
- query_grad: bfloat16 [2, 2048, 4096], P('dp', 'seq', 'head')
- key_grad: bfloat16 [2, 2048, 4096], P('dp', 'seq', 'head')
- value_grad: bfloat16 [2, 2048, 4096], P('dp', 'seq', 'head')
- gain_grad: float32 [4096], P('head')
Inputs may be any that keep to these rules, and one draw needn't show every extreme that they name: `lengths`: at least one response has length 2048.
All inputs are finite; a program needn't handle non-finite values. No bound on the sum of `loss_mask` on one device may be relied on, other than what follows from the above.
Results may differ from a plain program's by a relative error of at most 0.0063.
Values sent between devices are 32-bit elements; how exact they have to be, the bound alone decides.
A program may use at most 128 MiB of HBM per device.

v0:
```python
import jax
import jax.numpy as jnp
from jax import lax
from jax.sharding import PartitionSpec as P

clip_high = 1.28
epsilon = 1e-06


def on_device(
    query_rows,
    key_rows,
    value_rows,
    norm_gain,
    cotangent,
    loss_mask,
    importance,
    advantage,
    lengths,
    decay_index,
):
    batches, slab_len, features = query_rows.shape
    head_count = decay_index.shape[0]
    per_head = features // head_count
    seq_count = lax.axis_size("seq")
    seq_place = lax.axis_index("seq")
    decay_rate = 16.0 / (slab_len * jnp.exp2(decay_index.astype(jnp.float32)))
    query_heads = query_rows.reshape(batches, slab_len, head_count, per_head)
    key_heads = key_rows.reshape(batches, slab_len, head_count, per_head)
    value_heads = value_rows.reshape(batches, slab_len, head_count, per_head)
    offsets = jnp.arange(slab_len, dtype=jnp.float32)
    lagged = offsets[:, None] - offsets[None, :]
    within = jnp.where(
        lagged[None] >= 0,
        jnp.exp2(-decay_rate[:, None, None] * jnp.maximum(lagged, 0.0)[None]),
        0.0,
    )
    from_start = jnp.exp2(-decay_rate[None, :] * (offsets + 1.0)[:, None])
    to_next = jnp.exp2(-decay_rate[None, :] * (slab_len - offsets)[:, None])
    to_end = jnp.exp2(-decay_rate[None, :] * (slab_len - 1.0 - offsets)[:, None])
    from_begin = jnp.exp2(-decay_rate[None, :] * offsets[:, None])
    scores = jnp.einsum(
        "bthd,bshd->bhts", query_heads, key_heads, preferred_element_type=jnp.float32
    )
    score_half = (scores * within[None]).astype(jnp.bfloat16)
    local_out = jnp.einsum(
        "bhts,bshd->bthd", score_half, value_heads, preferred_element_type=jnp.float32
    )
    key_decayed = (key_heads.astype(jnp.float32) * to_end[None, :, :, None]).astype(jnp.bfloat16)
    state_local = jnp.einsum(
        "bthd,bthe->bhde", key_decayed, value_heads, preferred_element_type=jnp.float32
    )
    shards = lax.all_gather(state_local[None], "seq", axis=0, tiled=True)
    slab_ids = jnp.arange(shards.shape[0])
    distance = (seq_place - 1 - slab_ids).astype(jnp.float32)
    weight = jnp.where(
        (slab_ids < seq_place)[:, None],
        jnp.exp2(-decay_rate[None, :] * slab_len * jnp.maximum(distance, 0.0)[:, None]),
        0.0,
    )
    state_in = jnp.sum(weight[:, None, :, None, None] * shards, axis=0)
    state_half = state_in.astype(jnp.bfloat16)
    carried = jnp.einsum(
        "bthd,bhde->bthe", query_heads, state_half, preferred_element_type=jnp.float32
    )
    outputs_flat = (local_out + carried * from_start[None, :, :, None]).reshape(
        batches, slab_len, features
    )
    positions = seq_place * slab_len + jnp.arange(slab_len, dtype=jnp.int32)
    in_length = (positions[None, :] < lengths[:, None]).astype(jnp.float32)
    token_weight = loss_mask.astype(jnp.float32) * in_length * jnp.minimum(importance, clip_high)
    token_weight = (
        token_weight
        * advantage[:, None]
        * (float(slab_len * seq_count) / lengths.astype(jnp.float32))[:, None]
    )
    grad_y = cotangent.astype(jnp.float32) * token_weight[..., None]
    grad_n = grad_y * norm_gain
    statistics = lax.psum(
        (jnp.sum(outputs_flat * outputs_flat, -1), jnp.sum(grad_n * outputs_flat, -1)), "head"
    )
    total_features = features * lax.axis_size("head")
    inverse = lax.rsqrt(statistics[0] / total_features + epsilon)
    normed = outputs_flat * inverse[..., None]
    mixed = (normed * norm_gain).astype(jnp.bfloat16)
    mean_term = statistics[1] * inverse / total_features
    grad_out = (inverse[..., None] * (grad_n - normed * mean_term[..., None])).astype(jnp.bfloat16)
    gain_grad = lax.psum(jnp.sum(grad_y * normed, axis=(0, 1)), ("dp", "seq"))
    grad_heads = grad_out.reshape(batches, slab_len, head_count, per_head)
    dscore = jnp.einsum(
        "bthe,bshe->bhts", grad_heads, value_heads, preferred_element_type=jnp.float32
    )
    dscore = (dscore * within[None]).astype(jnp.bfloat16)
    query_decayed = (query_heads.astype(jnp.float32) * from_begin[None, :, :, None]).astype(
        jnp.bfloat16
    )
    return_local = jnp.einsum(
        "bthd,bthe->bhde", query_decayed, grad_heads, preferred_element_type=jnp.float32
    )
    shards = lax.all_gather(return_local[None], "seq", axis=0, tiled=True)
    slab_ids = jnp.arange(shards.shape[0])
    distance = (slab_ids - seq_place - 1).astype(jnp.float32)
    weight = jnp.where(
        (slab_ids > seq_place)[:, None],
        jnp.exp2(-decay_rate[None, :] * slab_len * jnp.maximum(distance, 0.0)[:, None]),
        0.0,
    )
    return_in = jnp.sum(weight[:, None, :, None, None] * shards, axis=0)
    return_half = return_in.astype(jnp.bfloat16)
    query_grad = jnp.einsum(
        "bhts,bshd->bthd", dscore, key_heads, preferred_element_type=jnp.float32
    )
    query_grad = (
        query_grad
        + jnp.einsum("bthe,bhde->bthd", grad_heads, state_half, preferred_element_type=jnp.float32)
        * from_start[None, :, :, None]
    )
    key_grad = jnp.einsum(
        "bhts,bthd->bshd", dscore, query_heads, preferred_element_type=jnp.float32
    )
    key_grad = (
        key_grad
        + jnp.einsum(
            "bthe,bhde->bthd", value_heads, return_half, preferred_element_type=jnp.float32
        )
        * to_next[None, :, :, None]
    )
    value_grad = jnp.einsum(
        "bhts,bthe->bshe", score_half, grad_heads, preferred_element_type=jnp.float32
    )
    value_grad = (
        value_grad
        + jnp.einsum("bthd,bhde->bthe", key_heads, return_half, preferred_element_type=jnp.float32)
        * to_next[None, :, :, None]
    )
    query_grad = query_grad.reshape(batches, slab_len, features).astype(jnp.bfloat16)
    key_grad = key_grad.reshape(batches, slab_len, features).astype(jnp.bfloat16)
    value_grad = value_grad.reshape(batches, slab_len, features).astype(jnp.bfloat16)
    return (mixed, query_grad, key_grad, value_grad, gain_grad)


def solution(mesh):
    in_specs = (
        P("dp", "seq", "head"),
        P("dp", "seq", "head"),
        P("dp", "seq", "head"),
        P("head"),
        P("dp", "seq", "head"),
        P("dp", "seq"),
        P("dp", "seq"),
        P("dp"),
        P("dp"),
        P("head"),
    )
    out_specs = (
        P("dp", "seq", "head"),
        P("dp", "seq", "head"),
        P("dp", "seq", "head"),
        P("dp", "seq", "head"),
        P("head"),
    )
    return jax.shard_map(
        on_device, mesh=mesh, in_specs=in_specs, out_specs=out_specs, check_vma=False
    )
```

profile of v0, /device:TPU:0, one launch (start us, length us, event | category | flops | bytes accessed | tf_op | source)
XLA Modules:
  0.0 140.8 jit_solution(556342294726366703)
XLA Ops:
  7.2 0.0 all-gather.5.cloned.1.call-start
  7.2 0.7 broadcast_multiply_fusion
  7.9 1.5 %copy.65 = bf16[64,8,8,128]{3,2,1,0:T(8,128)(2,1)S(1)} copy(bf16[64,8,8,128]{3,1,2,0:T(8,128)(2,1)} %bitcast.113) | data formatting | bytes 2097152
  9.4 0.7 copy.41
  10.1 1.9 %copy.66 = bf16[64,8,8,128]{3,2,1,0:T(8,128)(2,1)S(1)} copy(bf16[64,8,8,128]{3,1,2,0:T(8,128)(2,1)} %bitcast.114) | data formatting | bytes 2097152
  12.0 0.0 copy-start.4
  12.0 0.1 multiply_exponential_fusion
  12.1 1.3 fusion.8
  13.4 0.0 all-gather.5.cloned.1.call-update
  13.4 0.0 all-gather.7.cloned.1.call-start
  14.7 1.5 %copy.63 = bf16[1,512,1024]{1,2,0:T(8,128)(2,1)S(1)} copy(bf16[1,512,1024]{2,1,0:T(8,128)(2,1)} %param.10) | data formatting | bytes 2097152 | tf_op jit(solution)/shard_map/reshape
  16.3 0.3 fusion.13
  16.6 0.2 fusion.12
  16.8 0.0 copy-start.11
  16.8 0.1 exponential_select_fusion.1
  16.9 3.1 %multiply_convert_fusion.1 = bf16[8,512,512]{2,1,0:T(8,128)(2,1)S(1)} fusion(f32[512,512]{1,0:T(8,128)S(1)} %fusion.12, f32[8]{0:T(128)S(1)} %get-tuple-element.18, pred[512,512]{1,0:T(8,128)(4,1)S(1)} %fusion.13, bf16[512,8,128]{0,2,1:T(8,128)(2,1)S(1)} %bitcast.96, bf16[512,8,128]{2,1,0:T(8,128)(2,1)S(1)} %bitcast.101), kind=kOutput, calls=%fused_computation.1 | convolution fusion | flops 547356672 | bytes 7602208 | tf_op jit(solution)/shard_map/bthd,bshd->bhts/dot_general | solution.py:42
  20.1 1.9 %copy-done = bf16[8,512,512]{2,1,0:T(8,128)(2,1)} copy-done((bf16[8,512,512]{2,1,0:T(8,128)(2,1)}, bf16[8,512,512]{2,1,0:T(8,128)(2,1)S(1)}, u32[]{:S(2)}) %copy-start) | copy-done | bytes 4194328
  22.0 2.9 %fusion.16 = f32[8,512,128]{1,2,0:T(8,128)} fusion(bf16[8,512,512]{2,1,0:T(8,128)(2,1)S(1)} %multiply_convert_fusion.1, bf16[512,8,128]{2,1,0:T(8,128)(2,1)S(1)} %bitcast.104), kind=kOutput, calls=%fused_computation.34 | convolution fusion | flops 536870912 | bytes 7340032 | tf_op jit(solution)/shard_map/bhts,bshd->bthd/dot_general | solution.py:46
  24.9 26.6 %all-gather.5.cloned.1.call-done = f32[32,128,128]{2,1,0:T(8,128)} async-done(((f32[8,128,128]{2,1,0:T(8,128)}), f32[32,128,128]{2,1,0:T(8,128)}) %all-gather.5.cloned.1.call-update) | async-done | bytes 2097168 | tf_op jit(solution)/shard_map/all_gather | solution.py:53
  51.5 1.8 %multiply_reduce_fusion.4 = bf16[8,128,128]{2,1,0:T(8,128)(2,1)S(1)} fusion(f32[4,1,8,128,128]{4,3,2,0,1:T(8,128)} %bitcast.111, f32[4,8]{1,0:T(4,128)S(1)} %get-tuple-element.26), kind=kLoop, calls=%fused_computation.23 | loop fusion | flops 917504 | bytes 2359424 | tf_op jit(solution)/shard_map/reduce_sum | solution.py:61
  53.3 0.0 copy-done.6
  53.3 1.9 %multiply_reduce_fusion.3 = (f32[512]{0:T(512)S(1)}, f32[1,512,8,128]{1,3,2,0:T(8,128)}) fusion(f32[512,8]{0,1:T(8,128)S(1)} %get-tuple-element.24, bf16[8,128,128]{2,1,0:T(8,128)(2,1)S(1)} %multiply_reduce_fusion.4, bf16[512,8,128]{0,2,1:T(8,128)(2,1)S(1)} %bitcast.97, f32[8,512,128]{1,2,0:T(8,128)S(1)} %copy-done.6), kind=kOutput, calls=%fused_computation.22 | convolution fusion | flops 136314368 | bytes 5523456 | tf_op jit(solution)/shard_map/bthd,bhde->bthe/dot_general | solution.py:63
  55.2 11.7 %psum.21 = f32[1,512]{1,0:T(1,128)S(1)} all-reduce(f32[1,512]{1,0:T(1,128)S(1)} %bitcast.119), channel_id=1, replica_groups=mesh['dp'=2,'seq'=4,'head'=4] {'head'}, use_global_device_ids=true, to_apply=%region_2.3 | all-reduce | flops 512 | bytes 4096 | tf_op jit(solution)/shard_map/psum | solution.py:79
  66.8 1.9 %copy.45 = f32[1,512,1024]{2,1,0:T(8,128)S(1)} copy(f32[1,512,1024]{1,2,0:T(8,128)} %bitcast.107) | data formatting | bytes 4194304 | tf_op jit(solution)/shard_map/reshape | solution.py:66
  68.8 2.0 %multiply_reduce_fusion = (f32[1024]{0:T(1024)S(1)}, f32[512]{0:T(512)S(1)}) fusion(bf16[1,512,1024]{2,1,0:T(8,128)(2,1)} %param.14, f32[1,512,1024]{2,1,0:T(8,128)S(1)} %copy.45, f32[512]{0:T(512)S(1)} %bitcast.117, f32[512]{0:T(512)S(1)} %bitcast.115, f32[1024]{0:T(1024)S(1)} %copy-done.13), kind=kLoop, calls=%fused_computation.14 | loop fusion | flops 4192768 | bytes 3160064 | tf_op jit(solution)/shard_map/reduce_sum | solution.py:88
  70.8 8.4 %psum.22 = f32[1,512]{1,0:T(1,128)S(1)} all-reduce(f32[1,512]{1,0:T(1,128)S(1)} %bitcast.121), channel_id=1, replica_groups=mesh['dp'=2,'seq'=4,'head'=4] {'head'}, use_global_device_ids=true, to_apply=%region_4.5 | all-reduce | flops 512 | bytes 4096 | tf_op jit(solution)/shard_map/psum | solution.py:79
  79.1 3.2 %multiply_convert_fusion.3 = (bf16[1,512,1024]{2,1,0:T(8,128)(2,1)}, bf16[1,512,1024]{2,1,0:T(8,128)(2,1)}) fusion(bf16[1,512,1024]{2,1,0:T(8,128)(2,1)} %param.14, f32[1,512,1024]{2,1,0:T(8,128)S(1)} %copy.45, f32[512]{0:T(512)S(1)} %bitcast.120, f32[512]{0:T(512)S(1)} %bitcast.118, f32[1024]{0:T(1024)S(1)} %copy-done.13, f32[512]{0:T(512)S(1)} %bitcast.116), kind=kLoop, calls=%fused_computation.17 | loop fusion | flops 5242880 | bytes 5253120 | tf_op jit(solution)/shard_map/convert_element_type | solution.py:87
  82.4 1.5 %copy.64 = bf16[1,512,1024]{1,2,0:T(8,128)(2,1)S(1)} copy(bf16[1,512,1024]{2,1,0:T(8,128)(2,1)} %get-tuple-element.19) | data formatting | bytes 2097152 | tf_op jit(solution)/shard_map/reshape.38
  83.9 0.0 copy-start.5
  83.9 1.2 fusion.9
  85.1 0.0 all-gather.7.cloned.1.call-update
  85.1 0.0 copy-done.5
  85.2 0.0 copy-start.10
  85.2 4.2 %multiply_convert_fusion = bf16[8,512,512]{2,1,0:T(8,128)(2,1)S(1)} fusion(f32[512,512]{1,0:T(8,128)} %copy-done.11, f32[8]{0:T(128)S(1)} %get-tuple-element.18, pred[512,512]{1,0:T(8,128)(4,1)} %copy-done.12, bf16[512,8,128]{0,2,1:T(8,128)(2,1)S(1)} %bitcast.93, bf16[512,8,128]{2,1,0:T(8,128)(2,1)S(1)} %bitcast.105), kind=kOutput, calls=%fused_computation | convolution fusion | flops 547356672 | bytes 7602208 | tf_op jit(solution)/shard_map/bthe,bshe->bhts/dot_general | solution.py:90
  89.4 1.5 %fusion.27 = f32[8,512,128]{1,2,0:T(8,128)S(1)} fusion(bf16[8,512,512]{2,1,0:T(8,128)(2,1)S(1)} %multiply_convert_fusion, bf16[512,8,128]{0,2,1:T(8,128)(2,1)S(1)} %copy-done.10), kind=kOutput, calls=%fused_computation.64 | convolution fusion | flops 536870912 | bytes 7340032 | tf_op jit(solution)/shard_map/bhts,bshd->bthd/dot_general | solution.py:110
  90.9 0.5 copy-done.1
  91.4 1.4 %fusion.5 = bf16[1,512,8,128]{1,3,2,0:T(8,128)(2,1)} fusion(f32[8,512,128]{1,2,0:T(8,128)S(1)} %fusion.27, bf16[512,8,128]{0,2,1:T(8,128)(2,1)S(1)} %bitcast.94, f32[512,8]{0,1:T(8,128)S(1)} %get-tuple-element.24, bf16[8,128,128]{2,1,0:T(8,128)(2,1)S(1)} %multiply_reduce_fusion.4), kind=kOutput, calls=%fused_computation.11 | convolution fusion | flops 135790592 | bytes 4472832 | tf_op jit(solution)/shard_map/bthe,bhde->bthd/dot_general | solution.py:115
  92.8 2.3 %copy.58 = bf16[1,512,1024]{2,1,0:T(8,128)(2,1)} copy(bf16[1,512,1024]{1,2,0:T(8,128)(2,1)} %bitcast.108) | data formatting | bytes 2097152
  95.0 15.1 %psum.23 = f32[1024]{0:T(1024)} all-reduce(f32[1024]{0:T(1024)S(1)} %get-tuple-element.15), channel_id=1, replica_groups=mesh['dp'=2,'seq'=4,'head'=4] {'dp','seq'}, use_global_device_ids=true, to_apply=%region_7.8 | all-reduce | flops 1024 | bytes 8192 | tf_op jit(solution)/shard_map/psum | solution.py:88
  110.1 4.2 %fusion.28 = f32[8,128,512]{2,1,0:T(8,128)} fusion(bf16[512,8,128]{0,2,1:T(8,128)(2,1)S(1)} %bitcast.95, bf16[8,512,512]{2,1,0:T(8,128)(2,1)} %copy-done), kind=kOutput, calls=%fused_computation.65 | convolution fusion | flops 536870912 | bytes 7340032 | tf_op jit(solution)/shard_map/bhts,bthe->bshe/dot_general | solution.py:128
  114.4 5.0 %all-gather.7.cloned.1.call-done = f32[32,128,128]{2,1,0:T(8,128)} async-done(((f32[8,128,128]{2,1,0:T(8,128)}), f32[32,128,128]{2,1,0:T(8,128)}) %all-gather.7.cloned.1.call-update) | async-done | bytes 2097168 | tf_op jit(solution)/shard_map/all_gather | solution.py:100
  119.3 1.8 %multiply_reduce_fusion.1 = bf16[8,128,128]{2,1,0:T(8,128)(2,1)S(1)} fusion(f32[4,1,8,128,128]{4,3,2,0,1:T(8,128)} %bitcast.112, f32[4,8]{1,0:T(4,128)S(1)} %get-tuple-element.25), kind=kLoop, calls=%fused_computation.15 | loop fusion | flops 917504 | bytes 2359424 | tf_op jit(solution)/shard_map/reduce_sum | solution.py:108
  121.2 1.8 %fusion.18 = f32[8,128,512]{2,1,0:T(8,128)} fusion(bf16[512,8,128]{2,1,0:T(8,128)(2,1)S(1)} %bitcast.106, bf16[8,128,128]{2,1,0:T(8,128)(2,1)S(1)} %multiply_reduce_fusion.1), kind=kOutput, calls=%fused_computation.36 | convolution fusion | flops 134217728 | bytes 3407872 | tf_op jit(solution)/shard_map/bthe,bhde->bthd/dot_general | solution.py:123
  123.0 0.8 copy-done.7
  123.9 1.5 %fusion.1 = bf16[1,512,8,128]{1,3,2,0:T(8,128)(2,1)} fusion(f32[8,128,512]{2,1,0:T(8,128)S(1)} %copy-done.7, f32[512,8]{0,1:T(8,128)S(1)} %get-tuple-element.21, bf16[512,8,128]{2,1,0:T(8,128)(2,1)S(1)} %bitcast.102, bf16[8,128,128]{2,1,0:T(8,128)(2,1)S(1)} %multiply_reduce_fusion.1), kind=kOutput, calls=%fused_computation.5 | convolution fusion | flops 135790592 | bytes 4472832 | tf_op jit(solution)/shard_map/bthd,bhde->bthe/dot_general | solution.py:133
  125.4 2.4 %copy.60 = bf16[1,512,1024]{2,1,0:T(8,128)(2,1)} copy(bf16[1,512,1024]{1,2,0:T(8,128)(2,1)} %bitcast.109) | data formatting | bytes 2097152
  127.8 3.9 %fusion.3 = bf16[1,512,8,128]{1,3,2,0:T(8,128)(2,1)} fusion(f32[8,128,512]{2,1,0:T(8,128)S(1)} %copy-done.8, bf16[512,8,128]{0,2,1:T(8,128)(2,1)S(1)} %bitcast.99, bf16[8,512,512]{2,1,0:T(8,128)(2,1)} %copy-done.1, f32[512,8]{0,1:T(8,128)S(1)} %get-tuple-element.21), kind=kOutput, calls=%fused_computation.8 | convolution fusion | flops 538443776 | bytes 8404992 | tf_op jit(solution)/shard_map/bhts,bthd->bshd/dot_general | solution.py:118
  131.7 2.3 %copy.59 = bf16[1,512,1024]{2,1,0:T(8,128)(2,1)} copy(bf16[1,512,1024]{1,2,0:T(8,128)(2,1)} %bitcast.110) | data formatting | bytes 2097152
  (30 shorter events, 0.1 us)
Async XLA Ops:
  7.2 44.3 %all-gather.5.cloned.1.call-start = ((), (), s32[]{:S(2)}) async-start(), calls=%async_computation | async-start | bytes 2621440 | tf_op jit(solution)/shard_map/all_gather | solution.py:53
  9.4 7.5 %copy-start.2 = (bf16[64,8,8,128]{3,2,1,0:T(8,128)(2,1)}, bf16[64,8,8,128]{3,2,1,0:T(8,128)(2,1)S(1)}, u32[]{:S(2)}) copy-start(bf16[64,8,8,128]{3,2,1,0:T(8,128)(2,1)S(1)} %copy.65) | copy-start | bytes 3145732
  10.1 3.3 %copy-start.9 = (bf16[512,8,128]{0,2,1:T(8,128)(2,1)}, bf16[512,8,128]{0,2,1:T(8,128)(2,1)S(1)}, u32[]{:S(2)}) copy-start(bf16[512,8,128]{0,2,1:T(8,128)(2,1)S(1)} %copy.41) | copy-start | bytes 3145732
  12.0 8.0 %copy-start.4 = (bf16[64,8,8,128]{3,2,1,0:T(8,128)(2,1)}, bf16[64,8,8,128]{3,2,1,0:T(8,128)(2,1)S(1)}, u32[]{:S(2)}) copy-start(bf16[64,8,8,128]{3,2,1,0:T(8,128)(2,1)S(1)} %copy.66) | copy-start | bytes 3145732
  13.4 3.4 %copy-start.14 = (f32[1,512]{1,0:T(1,128)S(1)}, f32[1,512]{1,0:T(1,128)}, u32[]{:S(2)}) copy-start(f32[1,512]{1,0:T(1,128)} %param.16) | copy-start | bytes 6148
  13.4 3.4 %copy-start.15 = (s32[1,512]{1,0:T(1,128)S(1)}, s32[1,512]{1,0:T(1,128)}, u32[]{:S(2)}) copy-start(s32[1,512]{1,0:T(1,128)} %param.15) | copy-start | bytes 6148
  13.4 105.9 %all-gather.7.cloned.1.call-start = ((), (), s32[]{:S(2)}) async-start(), calls=%async_computation.1 | async-start | bytes 2621440 | tf_op jit(solution)/shard_map/all_gather | solution.py:100
  16.6 3.5 %copy-start.12 = (pred[512,512]{1,0:T(8,128)(4,1)}, pred[512,512]{1,0:T(8,128)(4,1)S(1)}, u32[]{:S(2)}) copy-start(pred[512,512]{1,0:T(8,128)(4,1)S(1)} %fusion.13) | copy-start | bytes 786436
  16.8 3.3 %copy-start.11 = (f32[512,512]{1,0:T(8,128)}, f32[512,512]{1,0:T(8,128)S(1)}, u32[]{:S(2)}) copy-start(f32[512,512]{1,0:T(8,128)S(1)} %fusion.12) | copy-start | bytes 3145732
  20.1 1.9 %copy-start = (bf16[8,512,512]{2,1,0:T(8,128)(2,1)}, bf16[8,512,512]{2,1,0:T(8,128)(2,1)S(1)}, u32[]{:S(2)}) copy-start(bf16[8,512,512]{2,1,0:T(8,128)(2,1)S(1)} %multiply_convert_fusion.1) | copy-start | bytes 12582916
  24.9 28.4 %copy-start.6 = (f32[8,512,128]{1,2,0:T(8,128)S(1)}, f32[8,512,128]{1,2,0:T(8,128)}, u32[]{:S(2)}) copy-start(f32[8,512,128]{1,2,0:T(8,128)} %fusion.16) | copy-start | bytes 6291460
  66.8 2.0 %copy-start.13 = (f32[1024]{0:T(1024)S(1)}, f32[1024]{0:T(1024)}, u32[]{:S(2)}) copy-start(f32[1024]{0:T(1024)} %param.13) | copy-start | bytes 12292
  83.9 1.3 copy-start.5
  85.2 4.2 %copy-start.10 = (bf16[512,8,128]{0,2,1:T(8,128)(2,1)S(1)}, bf16[512,8,128]{0,2,1:T(8,128)(2,1)}, u32[]{:S(2)}) copy-start(bf16[512,8,128]{0,2,1:T(8,128)(2,1)} %copy-done.9) | copy-start | bytes 3145732
  89.4 2.0 %copy-start.1 = (bf16[8,512,512]{2,1,0:T(8,128)(2,1)}, bf16[8,512,512]{2,1,0:T(8,128)(2,1)S(1)}, u32[]{:S(2)}) copy-start(bf16[8,512,512]{2,1,0:T(8,128)(2,1)S(1)} %multiply_convert_fusion) | copy-start | bytes 12582916
  121.2 1.8 %copy-start.3 = (bf16[64,8,8,128]{3,2,1,0:T(8,128)(2,1)S(1)}, bf16[64,8,8,128]{3,2,1,0:T(8,128)(2,1)}, u32[]{:S(2)}) copy-start(bf16[64,8,8,128]{3,2,1,0:T(8,128)(2,1)} %copy-done.2) | copy-start | bytes 3145732
  121.2 2.7 %copy-start.7 = (f32[8,128,512]{2,1,0:T(8,128)S(1)}, f32[8,128,512]{2,1,0:T(8,128)}, u32[]{:S(2)}) copy-start(f32[8,128,512]{2,1,0:T(8,128)} %fusion.28) | copy-start | bytes 6291460
  125.4 2.4 %copy-start.8 = (f32[8,128,512]{2,1,0:T(8,128)S(1)}, f32[8,128,512]{2,1,0:T(8,128)}, u32[]{:S(2)}) copy-start(f32[8,128,512]{2,1,0:T(8,128)} %fusion.18) | copy-start | bytes 6291460
Sparse Core Ops, SparseCore 0:
  13.5 37.8 all-gather.4
  85.3 34.0 all-gather.6
where the time goes:
time: 141 us
  blocking collectives  35.1 us (25%)
  waiting for transfers between devices  31.6 us (22%)
  matrix products  28.9 us (20%)
  local copies, waits for them, and re-layouts  19.2 us (14%)
  between operations  15.7 us (11%)
  other arithmetic  10.2 us (7%)
    all_gather x1, waiting for transfers between devices, on_device(): shards = lax.all_gather(state_local[None], 'seq', axis=0, tiled=True)  26.6 us
    psum x2, blocking collectives, on_device(): lax.psum((jnp.sum(outputs_flat * outputs_flat, -1), jnp.sum(grad_n * outp...  20 us
    psum x1, blocking collectives, on_device(): gain_grad = lax.psum(jnp.sum(grad_y * normed, axis=(0, 1)), ('dp', 'seq'))  15.1 us
    unnamed x37, local copies, waits for them, and re-layouts  13.6 us
    all_gather x1, waiting for transfers between devices, on_device(): shards = lax.all_gather(return_local[None], 'seq', axis=0, tiled=True)  4.96 us
    dot_general x1, matrix products, on_device(): jnp.einsum('bhts,bthe->bshe', score_half, grad_heads, preferred_element_t...  4.23 us
    dot_general x1, matrix products, on_device(): jnp.einsum('bthe,bshe->bhts', grad_heads, value_heads, preferred_element_...  4.18 us
    dot_general x1, matrix products, on_device(): jnp.einsum('bhts,bthd->bshd', dscore, query_heads, preferred_element_type...  3.89 us
  transfers between devices with their start and end apart: 2, of which 2 were waited for; matrix products, arithmetic and copies ran while one was open for 15% of the time, Pallas kernels for 0%

commit v1 on v0

v1 whole, which is shorter than its diff:
```python
import functools

import jax
import jax.numpy as jnp
from jax import lax
from jax.experimental import pallas as pl
from jax.experimental.pallas import tpu as pltpu
from jax.sharding import PartitionSpec as P

clip_high = 1.28
epsilon = 1e-06
f32 = jnp.float32
bf16 = jnp.bfloat16
MESH = pl.DeviceIdType.MESH


def dot(a, b, ca, cb):
    return lax.dot_general(a, b, (((ca,), (cb,)), ((), ())), preferred_element_type=f32)


def kernel(
    n_seq,
    n_head,
    n_dp,
    decay_ref,
    adv_ref,
    len_ref,
    gain_ref,
    mask_ref,
    imp_ref,
    q_hbm,
    k_hbm,
    v_hbm,
    c_hbm,
    o_mix,
    o_dq,
    o_dk,
    o_dv,
    gg_ref,
    q,
    k,
    v,
    c,
    out,
    go,
    pk,
    pv,
    probs,
    wtab,
    tot_f,
    rcv_f,
    tot_b,
    rcv_b,
    pref,
    state,
    stat,
    gsum,
    grcv,
    in_sem,
    fs_sem,
    fr_sem,
    bs_sem,
    br_sem,
    ss_sem,
    sr_sem,
    gs_sem,
    gr_sem,
):
    slab, features = q.shape
    heads = decay_ref.shape[0]
    dim = features // heads
    blk = min(256, slab)
    nblk = slab // blk
    stages = n_seq.bit_length() - 1
    me = lax.axis_index("seq")
    mh = lax.axis_index("head")
    md = lax.axis_index("dp")

    def partner(step):
        g = 1 << step
        bit = lax.rem(lax.div(me, g), 2)
        return me + g * (1 - 2 * bit)

    loads = [
        pltpu.make_async_copy(src.at[0], dst, in_sem.at[i])
        for i, (src, dst) in enumerate(((k_hbm, k), (v_hbm, v), (q_hbm, q), (c_hbm, c)))
    ]
    for load in loads:
        load.start()

    barrier = pltpu.get_barrier_semaphore()
    for s in range(stages):
        pl.semaphore_signal(barrier, inc=1, device_id={"seq": partner(s)}, device_id_type=MESH)
    for off in range(1, n_head):
        pl.semaphore_signal(
            barrier, inc=1, device_id={"head": lax.rem(mh + off, n_head)}, device_id_type=MESH
        )
    for off in range(1, n_dp):
        pl.semaphore_signal(
            barrier, inc=1, device_id={"dp": lax.rem(md + off, n_dp)}, device_id_type=MESH
        )
    pl.semaphore_wait(barrier, stages + n_head - 1 + n_dp - 1)

    def cols(h):
        return pl.ds(pl.multiple_of(h * dim, dim), dim)

    def rate(h, width):
        index = jnp.full((1, width), decay_ref[h], jnp.int32).astype(f32)
        return 16.0 / (slab * jnp.exp2(index))

    def rows_at(width):
        return lax.broadcasted_iota(jnp.int32, (slab, width), 0).astype(f32)

    def fwd_copy(s, h):
        return pltpu.make_async_remote_copy(
            src_ref=tot_f.at[s, h],
            dst_ref=rcv_f.at[s, h],
            send_sem=fs_sem.at[s, h],
            recv_sem=fr_sem.at[s, h],
            device_id={"seq": partner(s)},
            device_id_type=MESH,
        )

    def bwd_copy(s, h):
        return pltpu.make_async_remote_copy(
            src_ref=tot_b.at[s, h],
            dst_ref=rcv_b.at[s, h],
            send_sem=bs_sem.at[s, h],
            recv_sem=br_sem.at[s, h],
            device_id={"seq": partner(s)},
            device_id_type=MESH,
        )

    def merge(h, s, place, tot, rcv, first):
        g = 1 << s
        r = rate(h, dim) * slab
        upper = jnp.full((1, dim), lax.rem(lax.div(place, g), 2), jnp.int32).astype(f32)
        inner = jnp.full((1, dim), lax.rem(place, g), jnp.int32).astype(f32)
        got = rcv[s, h]
        to_prefix = upper * jnp.exp2(-r * inner)
        if first:
            pref[h] = to_prefix * got
        else:
            pref[h] = pref[h] + to_prefix * got
        if s + 1 < stages:
            whole = jnp.exp2(-r * g)
            from_got = upper * whole + (1.0 - upper)
            from_own = upper + (1.0 - upper) * whole
            tot[s + 1, h] = from_got * got + from_own * tot[s, h]

    loads[0].wait()
    loads[1].wait()

    @pl.loop(0, heads)
    def _(h):
        fade = jnp.exp2(-rate(h, dim) * (slab - 1.0 - rows_at(dim)))
        faded = (k[:, cols(h)].astype(f32) * fade).astype(bf16)
        tot_f[0, h] = dot(faded, v[:, cols(h)], 0, 0)
        fwd_copy(0, h).start()

    loads[2].wait()

    t_at = lax.broadcasted_iota(jnp.int32, (blk, blk), 0)
    s_at = lax.broadcasted_iota(jnp.int32, (blk, blk), 1)

    @pl.loop(0, heads)
    def _(h):
        r = rate(h, blk)
        near = jnp.exp2(-r * (t_at - s_at).astype(f32))
        wtab[h, 0] = jnp.where(t_at >= s_at, near, 0.0)
        for d in range(1, nblk):
            wtab[h, d] = near * jnp.exp2(-r * float(blk * d))
        for i in range(nblk):
            rows = pl.ds(i * blk, blk)
            total = None
            for j in range(i + 1):
                past = pl.ds(j * blk, blk)
                score = dot(q[rows, cols(h)], k[past, cols(h)], 1, 1)
                half = (score * wtab[h, i - j]).astype(bf16)
                probs[h, rows, past] = half
                part = dot(half, v[past, cols(h)], 1, 0)
                total = part if total is None else total + part
            out[rows, cols(h)] = total
        fwd_copy(0, h).wait()
        merge(h, 0, me, tot_f, rcv_f, True)
        if stages > 1:
            fwd_copy(1, h).start()

    for s in range(1, stages - 1):

        @pl.loop(0, heads)
        def _(h, s=s):
            fwd_copy(s, h).wait()
            merge(h, s, me, tot_f, rcv_f, False)
            fwd_copy(s + 1, h).start()

    loads[3].wait()

    token = mask_ref[...].astype(f32)
    at = me * slab + lax.broadcasted_iota(jnp.int32, (1, slab), 1)
    length = jnp.full((1, slab), len_ref[0], jnp.int32)
    token = token * (at < length).astype(f32) * jnp.minimum(imp_ref[...], clip_high)
    token = token * adv_ref[0] * (float(slab * n_seq) / length.astype(f32))

    def finish(h, carry):
        squares, mixes = carry
        if stages > 1:
            fwd_copy(stages - 1, h).wait()
            merge(h, stages - 1, me, tot_f, rcv_f, False)
        half = pref[h].astype(bf16)
        state[h] = half
        grow = jnp.exp2(-rate(h, dim) * (rows_at(dim) + 1.0))
        full = out[:, cols(h)] + dot(q[:, cols(h)], half, 1, 0) * grow
        out[:, cols(h)] = full
        gain = gain_ref[pl.ds(h, 1), :]
        return squares + full * full, mixes + c[:, cols(h)].astype(f32) * gain * full

    zeros = jnp.zeros((slab, dim), f32)
    squares, mixes = lax.fori_loop(0, heads, finish, (zeros, zeros))
    stat[mh, 0:1, :] = jnp.sum(squares.T, axis=0, keepdims=True)
    stat[mh, 1:2, :] = jnp.sum(mixes.T, axis=0, keepdims=True) * token
    sends = [
        pltpu.make_async_remote_copy(
            src_ref=stat.at[mh],
            dst_ref=stat.at[mh],
            send_sem=ss_sem.at[off - 1],
            recv_sem=sr_sem.at[off - 1],
            device_id={"head": lax.rem(mh + off, n_head)},
            device_id_type=MESH,
        )
        for off in range(1, n_head)
    ]
    for send in sends:
        send.start()
    for send in sends:
        send.wait()
    sums = stat[0]
    for i in range(1, n_head):
        sums = sums + stat[i]
    count = features * n_head
    inverse = lax.rsqrt(sums[0:1] / count + epsilon)
    mean = inverse * (sums[1:2] / count)

    def column(row):
        return jnp.broadcast_to(row, (dim, slab)).T

    inv_col = column(inverse)
    give_col = column(inverse * token)
    take_col = column(inverse * inverse * mean)

    @pl.loop(0, heads)
    def _(h):
        gain = gain_ref[pl.ds(h, 1), :]
        full = out[:, cols(h)]
        given = c[:, cols(h)].astype(f32) * give_col
        o_mix[0, :, cols(h)] = (full * inv_col * gain).astype(bf16)
        gsum[0, pl.ds(h, 1), :] = jnp.sum(given * full, axis=0, keepdims=True)
        grad = (given * gain - take_col * full).astype(bf16)
        go[:, cols(h)] = grad
        fade = jnp.exp2(-rate(h, dim) * rows_at(dim))
        faded = (q[:, cols(h)].astype(f32) * fade).astype(bf16)
        tot_b[0, h] = dot(faded, grad, 0, 0)
        bwd_copy(0, h).start()

    def gain_copy(s):
        target = {"dp": lax.rem(md + 1, n_dp)} if s == stages else {"seq": partner(s)}
        return pltpu.make_async_remote_copy(
            src_ref=gsum.at[s],
            dst_ref=grcv.at[s],
            send_sem=gs_sem.at[s],
            recv_sem=gr_sem.at[s],
            device_id=target,
            device_id_type=MESH,
        )

    gain_copy(0).start()
    back = n_seq - 1 - me

    @pl.loop(0, heads)
    def _(h):
        for i in range(nblk):
            rows = pl.ds(i * blk, blk)
            grad = go[rows, cols(h)]
            qi = q[rows, cols(h)]
            total = None
            for j in range(i + 1):
                past = pl.ds(j * blk, blk)
                score = dot(grad, v[past, cols(h)], 1, 1)
                half = (score * wtab[h, i - j]).astype(bf16)
                part = dot(half, k[past, cols(h)], 1, 0)
                total = part if total is None else total + part
                dk = dot(half, qi, 0, 0)
                dv = dot(probs[h, rows, past], grad, 0, 0)
                if j == i:
                    pk[past, cols(h)] = dk
                    pv[past, cols(h)] = dv
                else:
                    pk[past, cols(h)] += dk
                    pv[past, cols(h)] += dv
            grow = jnp.exp2(-rate(h, dim) * (rows_at(dim)[i * blk : (i + 1) * blk] + 1.0))
            total = total + dot(grad, state[h], 1, 1) * grow
            o_dq[0, rows, cols(h)] = total.astype(bf16)
        bwd_copy(0, h).wait()
        merge(h, 0, back, tot_b, rcv_b, True)
        if stages > 1:
            bwd_copy(1, h).start()

    rounds = stages + (1 if n_dp > 1 else 0)
    for s in range(rounds):
        gain_copy(s).wait()
        gsum[s + 1] = gsum[s] + grcv[s]
        if s + 1 < rounds:
            gain_copy(s + 1).start()
    gg_ref[...] = gsum[rounds]

    for s in range(1, stages - 1):

        @pl.loop(0, heads)
        def _(h, s=s):
            bwd_copy(s, h).wait()
            merge(h, s, back, tot_b, rcv_b, False)
            bwd_copy(s + 1, h).start()

    @pl.loop(0, heads)
    def _(h):
        if stages > 1:
            bwd_copy(stages - 1, h).wait()
            merge(h, stages - 1, back, tot_b, rcv_b, False)
        half = pref[h].astype(bf16)
        fade = jnp.exp2(-rate(h, dim) * (slab - rows_at(dim)))
        dk = pk[:, cols(h)] + dot(v[:, cols(h)], half, 1, 1) * fade
        o_dk[0, :, cols(h)] = dk.astype(bf16)
        dv = pv[:, cols(h)] + dot(k[:, cols(h)], half, 1, 0) * fade
        o_dv[0, :, cols(h)] = dv.astype(bf16)


def on_device(
    n_seq,
    n_head,
    n_dp,
    query_rows,
    key_rows,
    value_rows,
    norm_gain,
    cotangent,
    loss_mask,
    importance,
    advantage,
    lengths,
    decay_index,
):
    batches, slab, features = query_rows.shape
    heads = decay_index.shape[0]
    dim = features // heads
    stages = n_seq.bit_length() - 1
    assert batches == 1 and n_seq == 1 << stages and stages > 0 and n_dp <= 2
    vmem = pl.BlockSpec(memory_space=pltpu.VMEM)
    smem = pl.BlockSpec(memory_space=pltpu.SMEM)
    far = pl.BlockSpec(memory_space=pltpu.HBM)
    rows = jax.ShapeDtypeStruct(query_rows.shape, bf16)
    wide = pltpu.VMEM((slab, features), bf16)
    wide32 = pltpu.VMEM((slab, features), f32)
    blk = min(256, slab)
    states = pltpu.VMEM((stages, heads, dim, dim), f32)
    dma = pltpu.SemaphoreType.DMA
    mixed, dq, dk, dv, gain_grad = pl.pallas_call(
        functools.partial(kernel, n_seq, n_head, n_dp),
        out_shape=(rows, rows, rows, rows, jax.ShapeDtypeStruct((heads, dim), f32)),
        in_specs=[smem] * 3 + [vmem] * 3 + [far] * 4,
        out_specs=(vmem,) * 5,
        scratch_shapes=[wide] * 4
        + [wide32, wide, wide32, wide32]
        + [
            pltpu.VMEM((heads, slab, slab), bf16),
            pltpu.VMEM((heads, slab // blk, blk, blk), f32),
            states,
            states,
            states,
            states,
            pltpu.VMEM((heads, dim, dim), f32),
            pltpu.VMEM((heads, dim, dim), bf16),
            pltpu.VMEM((n_head, 2, slab), f32),
            pltpu.VMEM((stages + 2, heads, dim), f32),
            pltpu.VMEM((stages + 1, heads, dim), f32),
            dma((4,)),
            dma((stages, heads)),
            dma((stages, heads)),
            dma((stages, heads)),
            dma((stages, heads)),
            dma((max(n_head - 1, 1),)),
            dma((max(n_head - 1, 1),)),
            dma((stages + 1,)),
            dma((stages + 1,)),
        ],
        compiler_params=pltpu.CompilerParams(
            collective_id=0, has_side_effects=True, vmem_limit_bytes=48 << 20
        ),
        name="lightning",
    )(
        decay_index,
        advantage,
        lengths,
        norm_gain.reshape(heads, dim),
        loss_mask,
        importance,
        query_rows,
        key_rows,
        value_rows,
        cotangent,
    )
    return (mixed, dq, dk, dv, gain_grad.reshape(features))


def solution(mesh):
    wide = P("dp", "seq", "head")
    token = P("dp", "seq")
    in_specs = (wide, wide, wide, P("head"), wide, token, token, P("dp"), P("dp"), P("head"))
    out_specs = (wide, wide, wide, wide, P("head"))
    body = functools.partial(on_device, mesh.shape["seq"], mesh.shape["head"], mesh.shape["dp"])
    return jax.shard_map(
        body, mesh=mesh, in_specs=in_specs, out_specs=out_specs, check_vma=False
    )
```

time: 141 us -> 57 us (0.40)
  Pallas kernels: 0 us -> 47.1 us
  blocking collectives: 35.1 us -> 0 us
  waiting for transfers between devices: 31.6 us -> 0 us
  matrix products: 28.9 us -> 0 us
  between operations: 15.7 us -> 1.98 us
  local copies, waits for them, and re-layouts: 19.2 us -> 7.7 us
  other arithmetic: 10.2 us -> 0 us
    pallas_call x0 -> x1, Pallas kernels: none -> 47.1 us  [on_device(): pl.pallas_call(functools.partial(kernel, n_seq, n_head, n_dp), out_shape=...]
    psum x3 -> x0, blocking collectives: 35.1 us -> none  [the longest x2 20 us: on_device(): lax.psum((jnp.sum(outputs_flat * outputs_flat, -1), jnp.sum(grad_n * outp...]
    all_gather x2 -> x0, waiting for transfers between devices: 31.5 us -> none  [the longest x1 26.6 us: on_device(): shards = lax.all_gather(state_local[None], 'seq', axis=0, tiled=True)]
    dot_general x12 -> x0, matrix products: 28.9 us -> none  [the longest x1 4.23 us: on_device(): jnp.einsum('bhts,bthe->bshe', score_half, grad_heads, preferred_element_t...]
    unnamed x37 -> x15, local copies, waits for them, and re-layouts: 13.6 us -> 7.7 us
    reduce_sum x3 -> x0, other arithmetic: 5.63 us -> none  [the longest x1 1.97 us: on_device(): gain_grad = lax.psum(jnp.sum(grad_y * normed, axis=(0, 1)), ('dp', 'seq'))]
    reshape x2 -> x0, local copies, waits for them, and re-layouts: 3.43 us -> none  [the longest x1 1.93 us: on_device(): (local_out + carried * from_start[None, :, :, None]).reshape(batches, sla...]
    convert_element_type x1 -> x0, other arithmetic: 3.24 us -> none  [on_device(): (inverse[..., None] * (grad_n - normed * mean_term[..., None])).astype(jn...]
  transfers between devices with their start and end apart: 2 -> 0, of which waited for: 2 -> 0; matrix products, arithmetic and copies ran while one was open for 15% -> 0% of each run, Pallas kernels for 0% -> 0%
where the time goes in v1:
time: 57 us; the launch traced here: 56.7 us
  Pallas kernels  47.1 us (83%)
  local copies, waits for them, and re-layouts  7.7 us (14%)
  between operations  1.98 us (3%)
    pallas_call x1, Pallas kernels, on_device(): pl.pallas_call(functools.partial(kernel, n_seq, n_head, n_dp), out_shape=...  47.1 us
    unnamed x15, local copies, waits for them, and re-layouts  7.7 us

profile of v1, /device:TPU:0, one launch (start us, length us, event | category | flops | bytes accessed | tf_op | source)
XLA Modules:
  0.0 56.7 jit_solution(15644598265138853523)
XLA Ops:
  0.6 0.0 copy-start.1
  1.9 0.0 copy-start.4
  2.0 0.0 copy-done.1
  2.0 0.6 %copy-done.4 = s32[8]{0:T(128)S(1)} copy-done((s32[8]{0:T(128)S(1)}, s32[8]{0:T(128)}, u32[]{:S(2)}) %copy-start.4) | copy-done | bytes 56
  2.6 0.0 copy-start
  2.6 1.2 %copy-done = bf16[1,512,1024]{2,1,0:T(8,128)(2,1)S(1)} copy-done((bf16[1,512,1024]{2,1,0:T(8,128)(2,1)S(1)}, bf16[1,512,1024]{2,1,0:T(8,128)(2,1)}, u32[]{:S(2)}) %copy-start) | copy-done | bytes 1048600
  3.8 0.0 copy-start.2
  3.8 0.7 %copy-done.2 = s32[1,512]{1,0:T(1,128)S(1)} copy-done((s32[1,512]{1,0:T(1,128)S(1)}, s32[1,512]{1,0:T(1,128)}, u32[]{:S(2)}) %copy-start.2) | copy-done | bytes 2072
  4.5 0.0 copy-start.3
  4.5 0.7 %copy-done.3 = f32[1,512]{1,0:T(1,128)S(1)} copy-done((f32[1,512]{1,0:T(1,128)S(1)}, f32[1,512]{1,0:T(1,128)}, u32[]{:S(2)}) %copy-start.3) | copy-done | bytes 2072
  5.2 47.1 %lightning.1 = (bf16[1,512,1024]{2,1,0:T(8,128)(2,1)S(1)}, bf16[1,512,1024]{2,1,0:T(8,128)(2,1)S(1)}, bf16[1,512,1024]{2,1,0:T(8,128)(2,1)S(1)}, bf16[1,512,1024]{2,1,0:T(8,128)(2,1)S(1)}, f32[8,128]{1,0:T(8,128)S(1)}) custom-call(s32[8]{0:T(128)S(1)} %copy-done.4, f32[1]{0:T(128)S(6)} %copy.20.adv_ref, s32[1]{0:T(128)S(6)} %copy.21.len_ref, ...), custom_call_target="tpu_custom_call" | custom-call | tf_op jit(solution)/shard_map/lightning/pallas_call | solution.py:366
  52.3 1.0 %copy.22 = bf16[1,512,1024]{2,1,0:T(8,128)(2,1)} copy(bf16[1,512,1024]{2,1,0:T(8,128)(2,1)S(1)} %get-tuple-element.20) | data formatting | bytes 2097152
  53.2 1.0 %copy.23 = bf16[1,512,1024]{2,1,0:T(8,128)(2,1)} copy(bf16[1,512,1024]{2,1,0:T(8,128)(2,1)S(1)} %get-tuple-element.21) | data formatting | bytes 2097152
  54.2 1.0 %copy.24 = bf16[1,512,1024]{2,1,0:T(8,128)(2,1)} copy(bf16[1,512,1024]{2,1,0:T(8,128)(2,1)S(1)} %get-tuple-element.22) | data formatting | bytes 2097152
  55.2 1.0 %copy.25 = bf16[1,512,1024]{2,1,0:T(8,128)(2,1)} copy(bf16[1,512,1024]{2,1,0:T(8,128)(2,1)S(1)} %get-tuple-element.23) | data formatting | bytes 2097152
  56.2 0.6 %copy.26 = f32[1024]{0:T(1024)} copy(f32[1024]{0:T(1024)S(1)} %bitcast.3) | data formatting | bytes 8192
Async XLA Ops:
  0.6 1.3 %copy-start.1 = (f32[1024]{0:T(1024)S(1)}, f32[1024]{0:T(1024)}, u32[]{:S(2)}) copy-start(f32[1024]{0:T(1024)} %param.13) | copy-start | bytes 12292
  1.9 0.7 %copy-start.4 = (s32[8]{0:T(128)S(1)}, s32[8]{0:T(128)}, u32[]{:S(2)}) copy-start(s32[8]{0:T(128)} %decay_ref.1) | copy-start | bytes 100
  2.6 1.2 %copy-start = (bf16[1,512,1024]{2,1,0:T(8,128)(2,1)S(1)}, bf16[1,512,1024]{2,1,0:T(8,128)(2,1)}, u32[]{:S(2)}) copy-start(bf16[1,512,1024]{2,1,0:T(8,128)(2,1)} %q_hbm.1) | copy-start | bytes 3145732
  3.8 0.7 %copy-start.2 = (s32[1,512]{1,0:T(1,128)S(1)}, s32[1,512]{1,0:T(1,128)}, u32[]{:S(2)}) copy-start(s32[1,512]{1,0:T(1,128)} %mask_ref.1) | copy-start | bytes 6148
  4.5 0.7 %copy-start.3 = (f32[1,512]{1,0:T(1,128)S(1)}, f32[1,512]{1,0:T(1,128)}, u32[]{:S(2)}) copy-start(f32[1,512]{1,0:T(1,128)} %imp_ref.1) | copy-start | bytes 6148

commit v2 on v1

--- a/solution.py
+++ b/solution.py
@@ -22,12 +22,12 @@
     n_seq,
     n_head,
     n_dp,
-    decay_ref,
+    decay_hbm,
     adv_ref,
     len_ref,
-    gain_ref,
-    mask_ref,
-    imp_ref,
+    gain_hbm,
+    mask_hbm,
+    imp_hbm,
     q_hbm,
     k_hbm,
     v_hbm,
@@ -37,6 +37,10 @@
     o_dk,
     o_dv,
     gg_ref,
+    decay_ref,
+    gain_ref,
+    mask_ref,
+    imp_ref,
     q,
     k,
     v,
@@ -46,7 +50,12 @@
     pk,
     pv,
     probs,
+    dsc,
     wtab,
+    up,
+    down,
+    squares,
+    mixes,
     tot_f,
     rcv_f,
     tot_b,
@@ -57,6 +66,7 @@
     gsum,
     grcv,
     in_sem,
+    small_sem,
     fs_sem,
     fr_sem,
     bs_sem,
@@ -85,7 +95,18 @@
         pltpu.make_async_copy(src.at[0], dst, in_sem.at[i])
         for i, (src, dst) in enumerate(((k_hbm, k), (v_hbm, v), (q_hbm, q), (c_hbm, c)))
     ]
-    for load in loads:
+    small = [
+        pltpu.make_async_copy(src, dst, small_sem.at[i])
+        for i, (src, dst) in enumerate(
+            (
+                (decay_hbm, decay_ref),
+                (gain_hbm, gain_ref),
+                (mask_hbm, mask_ref),
+                (imp_hbm, imp_ref),
+            )
+        )
+    ]
+    for load in small + loads:
         load.start()
 
     barrier = pltpu.get_barrier_semaphore()
@@ -99,7 +120,6 @@
         pl.semaphore_signal(
             barrier, inc=1, device_id={"dp": lax.rem(md + off, n_dp)}, device_id_type=MESH
         )
-    pl.semaphore_wait(barrier, stages + n_head - 1 + n_dp - 1)
 
     def cols(h):
         return pl.ds(pl.multiple_of(h * dim, dim), dim)
@@ -108,8 +128,21 @@
         index = jnp.full((1, width), decay_ref[h], jnp.int32).astype(f32)
         return 16.0 / (slab * jnp.exp2(index))
 
-    def rows_at(width):
-        return lax.broadcasted_iota(jnp.int32, (slab, width), 0).astype(f32)
+    small[0].wait()
+    base = min(128, slab)
+    line = lax.broadcasted_iota(jnp.int32, (base, dim), 0).astype(f32)
+
+    @pl.loop(0, heads)
+    def _(h):
+        r = rate(h, dim)
+        rise = jnp.exp2(-r * line)
+        fall = jnp.exp2(-r * (base - 1.0 - line))
+        for b in range(slab // base):
+            rows = pl.ds(b * base, base)
+            up[h, rows, :] = rise * jnp.exp2(-r * float(b * base))
+            down[h, rows, :] = fall * jnp.exp2(-r * float(slab - (b + 1) * base))
+
+    pl.semaphore_wait(barrier, stages + n_head - 1 + n_dp - 1)
 
     def fwd_copy(s, h):
         return pltpu.make_async_remote_copy(
@@ -130,6 +163,48 @@
             device_id={"seq": partner(s)},
             device_id_type=MESH,
         )
+
+    def lower_only(s, place):
+        return lax.div(place, 2 << s) == n_seq // (2 << s) - 1
+
+    def is_upper(s, place):
+        return lax.rem(lax.div(place, 1 << s), 2) == 1
+
+    def sends(s, place):
+        return jnp.logical_not(jnp.logical_and(is_upper(s, place), lower_only(s, place)))
+
+    def takes(s, place):
+        return jnp.logical_or(is_upper(s, place), jnp.logical_not(lower_only(s, place)))
+
+    def begin(copy, s, h, place):
+        @pl.when(sends(s, place))
+        def _():
+            copy(s, h).start()
+
+    def settle(copy, place):
+        for s in range(stages):
+
+            @pl.when(sends(s, place))
+            def _(s=s):
+                @pl.loop(0, heads)
+                def _(h):
+                    copy(s, h).wait_send()
+
+    def accept(copy, h, s, place, tot, rcv):
+        first = s == 0
+        if first:
+
+            @pl.when(jnp.logical_not(takes(s, place)))
+            def _():
+                pref[h] = jnp.zeros((dim, dim), f32)
+
+        @pl.when(takes(s, place))
+        def _():
+            copy(s, h).wait_recv()
+            merge(h, s, place, tot, rcv, first)
+
+        if s + 1 < stages:
+            begin(copy, s + 1, h, place)
 
     def merge(h, s, place, tot, rcv, first):
         g = 1 << s
@@ -153,10 +228,9 @@
 
     @pl.loop(0, heads)
     def _(h):
-        fade = jnp.exp2(-rate(h, dim) * (slab - 1.0 - rows_at(dim)))
-        faded = (k[:, cols(h)].astype(f32) * fade).astype(bf16)
+        faded = (k[:, cols(h)].astype(f32) * down[h]).astype(bf16)
         tot_f[0, h] = dot(faded, v[:, cols(h)], 0, 0)
-        fwd_copy(0, h).start()
+        begin(fwd_copy, 0, h, me)
 
     loads[2].wait()
 
@@ -165,36 +239,35 @@
 
     @pl.loop(0, heads)
     def _(h):
-        r = rate(h, blk)
-        near = jnp.exp2(-r * (t_at - s_at).astype(f32))
+        r = rate(h, dim)
+        place = lax.broadcasted_iota(jnp.int32, (1, dim), 1).astype(f32)
+        front = up[h, pl.ds(0, blk), :]
+        near = jnp.concatenate(
+            [front * jnp.exp2(r * (place + float(b * dim))) for b in range(blk // dim)], axis=1
+        )
         wtab[h, 0] = jnp.where(t_at >= s_at, near, 0.0)
         for d in range(1, nblk):
-            wtab[h, d] = near * jnp.exp2(-r * float(blk * d))
+            far = jnp.exp2(-r * float(blk * d))
+            wtab[h, d] = near * jnp.concatenate([far] * (blk // dim), axis=1)
         for i in range(nblk):
             rows = pl.ds(i * blk, blk)
-            total = None
             for j in range(i + 1):
                 past = pl.ds(j * blk, blk)
                 score = dot(q[rows, cols(h)], k[past, cols(h)], 1, 1)
-                half = (score * wtab[h, i - j]).astype(bf16)
-                probs[h, rows, past] = half
-                part = dot(half, v[past, cols(h)], 1, 0)
-                total = part if total is None else total + part
-            out[rows, cols(h)] = total
-        fwd_copy(0, h).wait()
-        merge(h, 0, me, tot_f, rcv_f, True)
-        if stages > 1:
-            fwd_copy(1, h).start()
+                probs[h, rows, past] = (score * wtab[h, i - j]).astype(bf16)
+            past = pl.ds(0, (i + 1) * blk)
+            out[rows, cols(h)] = dot(probs[h, rows, past], v[past, cols(h)], 1, 0)
+        accept(fwd_copy, h, 0, me, tot_f, rcv_f)
 
     for s in range(1, stages - 1):
 
         @pl.loop(0, heads)
         def _(h, s=s):
-            fwd_copy(s, h).wait()
-            merge(h, s, me, tot_f, rcv_f, False)
-            fwd_copy(s + 1, h).start()
+            accept(fwd_copy, h, s, me, tot_f, rcv_f)
 
     loads[3].wait()
+    for load in small[1:]:
+        load.wait()
 
     token = mask_ref[...].astype(f32)
     at = me * slab + lax.broadcasted_iota(jnp.int32, (1, slab), 1)
@@ -202,24 +275,25 @@
     token = token * (at < length).astype(f32) * jnp.minimum(imp_ref[...], clip_high)
     token = token * adv_ref[0] * (float(slab * n_seq) / length.astype(f32))
 
-    def finish(h, carry):
-        squares, mixes = carry
+    squares[...] = jnp.zeros((slab, dim), f32)
+    mixes[...] = jnp.zeros((slab, dim), f32)
+
+    @pl.loop(0, heads)
+    def _(h):
         if stages > 1:
-            fwd_copy(stages - 1, h).wait()
-            merge(h, stages - 1, me, tot_f, rcv_f, False)
+            accept(fwd_copy, h, stages - 1, me, tot_f, rcv_f)
         half = pref[h].astype(bf16)
         state[h] = half
-        grow = jnp.exp2(-rate(h, dim) * (rows_at(dim) + 1.0))
+        grow = up[h] * jnp.exp2(-rate(h, dim))
         full = out[:, cols(h)] + dot(q[:, cols(h)], half, 1, 0) * grow
         out[:, cols(h)] = full
         gain = gain_ref[pl.ds(h, 1), :]
-        return squares + full * full, mixes + c[:, cols(h)].astype(f32) * gain * full
-
-    zeros = jnp.zeros((slab, dim), f32)
-    squares, mixes = lax.fori_loop(0, heads, finish, (zeros, zeros))
-    stat[mh, 0:1, :] = jnp.sum(squares.T, axis=0, keepdims=True)
-    stat[mh, 1:2, :] = jnp.sum(mixes.T, axis=0, keepdims=True) * token
-    sends = [
+        squares[...] += full * full
+        mixes[...] += c[:, cols(h)].astype(f32) * gain * full
+
+    stat[mh, 0:1, :] = jnp.sum(squares[...].T, axis=0, keepdims=True)
+    stat[mh, 1:2, :] = jnp.sum(mixes[...].T, axis=0, keepdims=True) * token
+    posts = [
         pltpu.make_async_remote_copy(
             src_ref=stat.at[mh],
             dst_ref=stat.at[mh],
@@ -230,10 +304,11 @@
         )
         for off in range(1, n_head)
     ]
-    for send in sends:
-        send.start()
-    for send in sends:
-        send.wait()
+    for post in posts:
+        post.start()
+    settle(fwd_copy, me)
+    for post in posts:
+        post.wait()
     sums = stat[0]
     for i in range(1, n_head):
         sums = sums + stat[i]
@@ -244,6 +319,7 @@
     def column(row):
         return jnp.broadcast_to(row, (dim, slab)).T
 
+    back = n_seq - 1 - me
     inv_col = column(inverse)
     give_col = column(inverse * token)
     take_col = column(inverse * inverse * mean)
@@ -257,10 +333,9 @@
         gsum[0, pl.ds(h, 1), :] = jnp.sum(given * full, axis=0, keepdims=True)
         grad = (given * gain - take_col * full).astype(bf16)
         go[:, cols(h)] = grad
-        fade = jnp.exp2(-rate(h, dim) * rows_at(dim))
-        faded = (q[:, cols(h)].astype(f32) * fade).astype(bf16)
+        faded = (q[:, cols(h)].astype(f32) * up[h]).astype(bf16)
         tot_b[0, h] = dot(faded, grad, 0, 0)
-        bwd_copy(0, h).start()
+        begin(bwd_copy, 0, h, back)
 
     def gain_copy(s):
         target = {"dp": lax.rem(md + 1, n_dp)} if s == stages else {"seq": partner(s)}
@@ -274,36 +349,27 @@
         )
 
     gain_copy(0).start()
-    back = n_seq - 1 - me
 
     @pl.loop(0, heads)
     def _(h):
         for i in range(nblk):
             rows = pl.ds(i * blk, blk)
             grad = go[rows, cols(h)]
-            qi = q[rows, cols(h)]
-            total = None
             for j in range(i + 1):
                 past = pl.ds(j * blk, blk)
                 score = dot(grad, v[past, cols(h)], 1, 1)
-                half = (score * wtab[h, i - j]).astype(bf16)
-                part = dot(half, k[past, cols(h)], 1, 0)
-                total = part if total is None else total + part
-                dk = dot(half, qi, 0, 0)
-                dv = dot(probs[h, rows, past], grad, 0, 0)
-                if j == i:
-                    pk[past, cols(h)] = dk
-                    pv[past, cols(h)] = dv
-                else:
-                    pk[past, cols(h)] += dk
-                    pv[past, cols(h)] += dv
-            grow = jnp.exp2(-rate(h, dim) * (rows_at(dim)[i * blk : (i + 1) * blk] + 1.0))
+                dsc[rows, past] = (score * wtab[h, i - j]).astype(bf16)
+            past = pl.ds(0, (i + 1) * blk)
+            grow = up[h, rows, :] * jnp.exp2(-rate(h, dim))
+            total = dot(dsc[rows, past], k[past, cols(h)], 1, 0)
             total = total + dot(grad, state[h], 1, 1) * grow
             o_dq[0, rows, cols(h)] = total.astype(bf16)
-        bwd_copy(0, h).wait()
-        merge(h, 0, back, tot_b, rcv_b, True)
-        if stages > 1:
-            bwd_copy(1, h).start()
+        for j in range(nblk):
+            past = pl.ds(j * blk, blk)
+            rest = pl.ds(j * blk, slab - j * blk)
+            pk[past, cols(h)] = dot(dsc[rest, past], q[rest, cols(h)], 0, 0)
+            pv[past, cols(h)] = dot(probs[h, rest, past], go[rest, cols(h)], 0, 0)
+        accept(bwd_copy, h, 0, back, tot_b, rcv_b)
 
     rounds = stages + (1 if n_dp > 1 else 0)
     for s in range(rounds):
@@ -317,21 +383,29 @@
 
         @pl.loop(0, heads)
         def _(h, s=s):
-            bwd_copy(s, h).wait()
-            merge(h, s, back, tot_b, rcv_b, False)
-            bwd_copy(s + 1, h).start()
+            accept(bwd_copy, h, s, back, tot_b, rcv_b)
 
     @pl.loop(0, heads)
     def _(h):
         if stages > 1:
-            bwd_copy(stages - 1, h).wait()
-            merge(h, stages - 1, back, tot_b, rcv_b, False)
+            accept(bwd_copy, h, stages - 1, back, tot_b, rcv_b)
         half = pref[h].astype(bf16)
-        fade = jnp.exp2(-rate(h, dim) * (slab - rows_at(dim)))
+        fade = down[h] * jnp.exp2(-rate(h, dim))
         dk = pk[:, cols(h)] + dot(v[:, cols(h)], half, 1, 1) * fade
         o_dk[0, :, cols(h)] = dk.astype(bf16)
         dv = pv[:, cols(h)] + dot(k[:, cols(h)], half, 1, 0) * fade
         o_dv[0, :, cols(h)] = dv.astype(bf16)
+
+    settle(bwd_copy, back)
+
+
+def writer(n, *refs):
+    sem = refs[-1]
+    copies = [pltpu.make_async_copy(refs[i], refs[n + i], sem.at[i]) for i in range(n)]
+    for copy in copies:
+        copy.start()
+    for copy in copies:
+        copy.wait()
 
 
 def on_device(
@@ -363,16 +437,31 @@
     blk = min(256, slab)
     states = pltpu.VMEM((stages, heads, dim, dim), f32)
     dma = pltpu.SemaphoreType.DMA
-    mixed, dq, dk, dv, gain_grad = pl.pallas_call(
+
+    def stay(array):
+        return pltpu.with_memory_space_constraint(array, pltpu.HBM)
+
+    results = pl.pallas_call(
         functools.partial(kernel, n_seq, n_head, n_dp),
         out_shape=(rows, rows, rows, rows, jax.ShapeDtypeStruct((heads, dim), f32)),
-        in_specs=[smem] * 3 + [vmem] * 3 + [far] * 4,
+        in_specs=[far, smem, smem] + [far] * 7,
         out_specs=(vmem,) * 5,
-        scratch_shapes=[wide] * 4
+        scratch_shapes=[
+            pltpu.SMEM((heads,), jnp.int32),
+            pltpu.VMEM((heads, dim), f32),
+            pltpu.VMEM((1, slab), jnp.int32),
+            pltpu.VMEM((1, slab), f32),
+        ]
+        + [wide] * 4
         + [wide32, wide, wide32, wide32]
         + [
             pltpu.VMEM((heads, slab, slab), bf16),
+            pltpu.VMEM((slab, slab), bf16),
             pltpu.VMEM((heads, slab // blk, blk, blk), f32),
+            pltpu.VMEM((heads, slab, dim), f32),
+            pltpu.VMEM((heads, slab, dim), f32),
+            pltpu.VMEM((slab, dim), f32),
+            pltpu.VMEM((slab, dim), f32),
             states,
             states,
             states,
@@ -382,6 +471,7 @@
             pltpu.VMEM((n_head, 2, slab), f32),
             pltpu.VMEM((stages + 2, heads, dim), f32),
             pltpu.VMEM((stages + 1, heads, dim), f32),
+            dma((4,)),
             dma((4,)),
             dma((stages, heads)),
             dma((stages, heads)),
@@ -397,17 +487,28 @@
         ),
         name="lightning",
     )(
-        decay_index,
+        stay(decay_index),
         advantage,
         lengths,
-        norm_gain.reshape(heads, dim),
-        loss_mask,
-        importance,
-        query_rows,
-        key_rows,
-        value_rows,
-        cotangent,
+        stay(norm_gain.reshape(heads, dim)),
+        stay(loss_mask),
+        stay(importance),
+        stay(query_rows),
+        stay(key_rows),
+        stay(value_rows),
+        stay(cotangent),
     )
+    shapes = tuple(jax.ShapeDtypeStruct(r.shape, r.dtype) for r in results)
+    any_space = pl.BlockSpec(memory_space=pl.ANY)
+    mixed, dq, dk, dv, gain_grad = pl.pallas_call(
+        functools.partial(writer, len(shapes)),
+        out_shape=shapes,
+        in_specs=[vmem] * len(shapes),
+        out_specs=(any_space,) * len(shapes),
+        scratch_shapes=[dma((len(shapes),))],
+        compiler_params=pltpu.CompilerParams(vmem_limit_bytes=8 << 20),
+        name="writer",
+    )(*results)
     return (mixed, dq, dk, dv, gain_grad.reshape(features))
 
 

time: 57 us -> 49.4 us (0.87)
  local copies, waits for them, and re-layouts: 7.7 us -> 0 us
    unnamed x15 -> x0, local copies, waits for them, and re-layouts: 7.7 us -> none
    pallas_call x0 -> x1, Pallas kernels: none -> 2.05 us  [on_device(): pl.pallas_call(functools.partial(writer, len(shapes)), out_shape=shapes,...]
    pallas_call x1, Pallas kernels: 47.1 us -> 45.3 us  [on_device(): pl.pallas_call(functools.partial(kernel, n_seq, n_head, n_dp), out_shape=...]
where the time goes in v2:
time: 49.4 us; the launch traced here: 49.3 us
  Pallas kernels  47.3 us (96%)
  between operations  1.93 us (4%)
    pallas_call x1, Pallas kernels, on_device(): pl.pallas_call(functools.partial(kernel, n_seq, n_head, n_dp), out_shape=...  45.3 us
    pallas_call x1, Pallas kernels, on_device(): pl.pallas_call(functools.partial(writer, len(shapes)), out_shape=shapes,...  2.05 us

profile of v2, /device:TPU:0, one launch (start us, length us, event | category | flops | bytes accessed | tf_op | source)
XLA Modules:
  0.0 49.3 jit_solution(9504408903047888413)
XLA Ops:
  1.9 45.3 %lightning.1 = (bf16[1,512,1024]{2,1,0:T(8,128)(2,1)S(1)}, bf16[1,512,1024]{2,1,0:T(8,128)(2,1)S(1)}, bf16[1,512,1024]{2,1,0:T(8,128)(2,1)S(1)}, bf16[1,512,1024]{2,1,0:T(8,128)(2,1)S(1)}, f32[8,128]{1,0:T(8,128)S(1)}) custom-call(s32[8]{0:T(128)} %decay_hbm.1, f32[1]{0:T(128)S(6)} %copy.15.adv_ref, s32[1]{0:T(128)S(6)} %copy.16.len_ref, f32[8,128]{1,0:T(8,128)} %bitcast.2, ...), custom_call_target="tpu_custom_call" | custom-call | tf_op jit(solution)/shard_map/lightning/pallas_call | solution.py:444
  47.2 2.1 %writer.1 = (bf16[1,512,1024]{2,1,0:T(8,128)(2,1)}, bf16[1,512,1024]{2,1,0:T(8,128)(2,1)}, bf16[1,512,1024]{2,1,0:T(8,128)(2,1)}, bf16[1,512,1024]{2,1,0:T(8,128)(2,1)}, f32[8,128]{1,0:T(8,128)}) custom-call(bf16[1,512,1024]{2,1,0:T(8,128)(2,1)S(1)} %get-tuple-element.15.refs_0_, bf16[1,512,1024]{2,1,0:T(8,128)(2,1)S(1)} %get-tuple-element.16.refs_1_, ...), custom_call_target="tpu_custom_call" | custom-call | tf_op jit(solution)/shard_map/writer/pallas_call | solution.py:503
